TPU v7x, 128 devices: a whole 4x4x4 slice. The times are simulated.
128 devices in a mesh: inp: 8 (over z, x_hi), tm: 8 (over x_lo, y), bl: 2 (over core).
Axes of the slice: x: 4 (x_hi: 2, x_lo: 2; x = x_hi * 2 + x_lo), y: 4, z: 4, core: 2. Of those that a mesh axis runs over, the one named last changes fastest.
Arguments:
- voltages: int32 [1024, 524288], P(('inp', 'bl'), 'tm'), may hold values from -16 to 14, as said below
- taps: float32 [4, 16384], replicated, may hold values from -3 to 3
- flags: int32 [1024], P(('inp', 'bl')), may hold values 0 or 1
Outputs:
- visibilities: float32 [2, 128, 8, 128, 1024], P(None, ('inp', 'tm'), None, 'bl')
Inputs may be any that keep to these rules, and one draw needn't show every extreme that they name: `voltages`: int8-valued digitized samples, each input's stream in time order.
All inputs are finite; a program needn't handle non-finite values. No bound on the sum of `flags` on one device may be relied on, other than what follows from the above.
Results may differ from a plain program's by a relative error of at most 0.00065.
Values may be sent and summed in bfloat16 or wider, within the bound.
A program may use at most 192 MiB of HBM per device.

v0:
```python
import math
import jax
import jax.numpy as jnp
from jax import lax
from jax.sharding import PartitionSpec as P

CH_AVG = 64


def passed_along(value, axis, steps):
    count = lax.axis_size(axis)
    initial, last = (max(0, -steps), min(count, count - steps))
    return lax.ppermute(value, axis, [(source, source + steps) for source in range(initial, last)])


def cos_sin(height, breadth, period):
    grid = lax.broadcasted_iota(jnp.int32, (height, breadth), 0) * lax.broadcasted_iota(
        jnp.int32, (height, breadth), 1
    )
    angle = (grid % period).astype(jnp.float32) * (2.0 * math.pi / period)
    return (jnp.cos(angle), jnp.sin(angle))


def transform(filtered, length):
    batch = filtered.shape[0]
    first_len = 128
    second_len = length // first_len
    highest = lax.Precision.HIGHEST
    blocks = filtered.reshape(batch, first_len, second_len)
    cos_one, sin_one = cos_sin(first_len, first_len, first_len)
    table_one = jnp.stack([cos_one, -sin_one])
    section_one = jnp.einsum("ykn,mnb->mykb", table_one, blocks, precision=highest)
    cos_twist, sin_twist = cos_sin(first_len, second_len, length)
    real_one = section_one[:, 0]
    imag_one = section_one[:, 1]
    twisted = jnp.stack(
        [real_one * cos_twist + imag_one * sin_twist, imag_one * cos_twist - real_one * sin_twist],
        axis=1,
    )
    cos_two, sin_two = cos_sin(second_len, second_len // 2, second_len)
    table_two = jnp.stack(
        [jnp.stack([cos_two, -sin_two], axis=1), jnp.stack([sin_two, cos_two], axis=1)]
    )
    result = jnp.einsum("mxkb,xbyq->ymqk", twisted, table_two, precision=highest)
    return result.reshape(2, batch, length // 2)


def shards(voltages, taps, flags):
    inputs = voltages.shape[0]
    tap_count = taps.shape[0]
    length = taps.shape[1]
    spectra_dev = voltages.shape[1] // length
    reach = tap_count - 1
    samples = voltages.astype(jnp.float32).reshape(inputs, spectra_dev, length)
    leading = voltages[:, : reach * length].reshape(inputs, reach, length).astype(jnp.bfloat16)
    following = passed_along(leading, "tm", -1)
    extended = jnp.concatenate([samples, following.astype(jnp.float32)], axis=1)
    filtered = jnp.zeros((inputs, spectra_dev, length), jnp.float32)
    for offset in range(tap_count):
        filtered = (
            filtered + taps[offset][None, None, :] * extended[:, offset : offset + spectra_dev]
        )
    channels = length // 2
    both_parts = transform(filtered.reshape(inputs * spectra_dev, length), length)
    scale = flags.astype(jnp.float32)[None, :, None, None] / (8.0 * math.sqrt(length))
    spectra = (both_parts.reshape(2, inputs, spectra_dev, channels) * scale).astype(jnp.bfloat16)
    turned = lax.all_to_all(
        spectra[:, None], ("inp", "tm"), split_axis=4, concat_axis=1, tiled=True
    )
    groups_inp = lax.axis_size("inp")
    groups_tm = lax.axis_size("tm")
    local_channels = channels // (groups_inp * groups_tm)
    out_groups = local_channels // CH_AVG
    rows = turned.reshape(2, groups_inp, groups_tm, inputs, spectra_dev, out_groups, CH_AVG)
    count = float(groups_tm * spectra_dev * CH_AVG)
    products = jnp.einsum(
        "xatisgk,yctjsgk->gxyaicj",
        rows,
        lax.all_gather(rows, "bl", axis=3, tiled=True),
        preferred_element_type=jnp.float32,
    )
    real_vis = products[:, 0, 0] + products[:, 1, 1]
    imag_vis = products[:, 1, 0] - products[:, 0, 1]
    visibilities = jnp.stack([real_vis, imag_vis]) / count
    return visibilities.reshape(
        2, out_groups, groups_inp, inputs, groups_inp * inputs * lax.axis_size("bl")
    )


def solution(mesh):
    in_specs = (P(("inp", "bl"), "tm"), P(), P(("inp", "bl")))
    out_specs = P(None, ("inp", "tm"), None, "bl", None)
    return jax.shard_map(shards, mesh=mesh, in_specs=in_specs, out_specs=out_specs, check_vma=False)
```

profile of v0, /device:TPU:1, one launch (start us, length us, event | category | flops | bytes accessed | tf_op | source)
XLA Modules:
  0.0 725.3 jit_solution(16236080894492939012)
XLA Ops:
  6.5 5.2 slice_convert_fusion
  16.2 11.3 %convert_element_type.80 = f32[64,65536]{1,0:T(8,128)} convert(s32[64,65536]{1,0:T(8,128)} %param.3) | non-fusion elementwise | flops 4194304 | bytes 33554432 | tf_op jit(solution)/shard_map/convert_element_type | solution.py:54
  27.5 17.6 %reshape.218 = f32[64,4,16384]{2,1,0:T(4,128)} reshape(f32[64,65536]{1,0:T(8,128)} %convert_element_type.80) | data formatting | bytes 33554432 | tf_op jit(solution)/shard_map/reshape | solution.py:54
  46.2 107.9 %collective-permute-done = bf16[64,3,16384]{2,0,1:T(8,128)(2,1)} collective-permute-done((bf16[64,3,16384]{2,0,1:T(8,128)(2,1)}, bf16[64,3,16384]{2,0,1:T(8,128)(2,1)}, u32[]{:S(2)}, u32[]{:S(2)}) %collective-permute-start) | collective-permute-done | bytes 6291488 | tf_op jit(solution)/shard_map/ppermute | solution.py:13
  154.1 11.2 %copy.53 = f32[64,3,16384]{2,1,0:T(4,128)} copy(bf16[64,3,16384]{2,0,1:T(8,128)(2,1)} %collective-permute-done) | data formatting | bytes 18874368 | tf_op jit(solution)/shard_map/convert_element_type | solution.py:57
  165.3 32.6 %fusion.8 = f32[64,4,16384]{2,1,0:T(4,128)} fusion(f32[64,4,16384]{2,1,0:T(4,128)S(1)} %copy-done, f32[64,3,16384]{2,1,0:T(4,128)} %copy.53, f32[16384]{0:T(1024)S(1)} %bitcast.77, f32[16384]{0:T(1024)S(1)} %bitcast.78, f32[16384]{0:T(1024)S(1)} %bitcast.76, f32[16384]{0:T(1024)S(1)} %bitcast.75), kind=kLoop, calls=%fused_computation.13 | loop fusion | flops 41943040 | bytes 46399488 | tf_op jit(solution)/shard_map/add | solution.py:61
  197.9 20.5 %reshape_reshape.6 = f32[256,128,128]{2,1,0:T(8,128)} reshape(f32[64,4,16384]{2,1,0:T(4,128)} %fusion.8) | data formatting | bytes 33554432 | tf_op jit(solution)/shard_map/reshape;reshape | solution.py:29
  218.4 32.5 %fusion.17 = f32[256,2,128,128]{2,3,1,0:T(8,128)} fusion(f32[256,128,128]{2,1,0:T(8,128)} %reshape_reshape.6, f32[1,128,128]{2,1,0:T(8,128)S(1)} %get-tuple-element.15, f32[1,128,128]{2,1,0:T(8,128)S(1)} %get-tuple-element.16), kind=kOutput, calls=%fused_computation.26 | convolution fusion | flops 12884934656 | bytes 50462720 | tf_op jit(solution)/shard_map/ykn,mnb->mykb/dot_general | solution.py:32
  250.8 17.8 %multiply_add_fusion = (f32[256,1,128,128]{2,3,1,0:T(8,128)S(1)}, f32[256,1,128,128]{2,3,1,0:T(8,128)}) fusion(f32[256,2,128,128]{2,3,1,0:T(8,128)} %fusion.17, f32[128,128]{0,1:T(8,128)S(1)} %get-tuple-element.17, f32[128,128]{0,1:T(8,128)S(1)} %get-tuple-element.18), kind=kLoop, calls=%fused_computation.25 | loop fusion | flops 25165824 | bytes 67239936 | tf_op jit(solution)/shard_map/add | solution.py:37
  268.6 23.6 %fusion.25 = f32[2,256,64,128]{3,2,1,0:T(8,128)} fusion(f32[256,1,128,128]{2,3,1,0:T(8,128)} %get-tuple-element.6, f32[256,1,128,128]{2,3,1,0:T(8,128)S(1)} %get-tuple-element.5, f32[1,128,2,64]{1,3,0,2:T(8,128)S(1)} %get-tuple-element.14, f32[1,128,2,64]{1,3,0,2:T(8,128)S(1)} %get-tuple-element.13), kind=kOutput, calls=%fused_computation.30 | convolution fusion | flops 12893323264 | bytes 50462720 | tf_op jit(solution)/shard_map/mxkb,xbyq->ymqk/dot_general | solution.py:44
  292.2 19.9 %reshape_reshape.7 = f32[2,1,64,4,8192]{4,3,2,0,1:T(4,128)} reshape(f32[2,256,64,128]{3,2,1,0:T(8,128)} %fusion.25) | data formatting | bytes 33554432 | tf_op jit(solution)/shard_map/reshape;reshape | solution.py:66
  312.2 16.6 %fusion.16 = bf16[2,1,64,4,8192]{4,2,3,1,0:T(8,128)(2,1)} fusion(f32[2,1,64,4,8192]{4,3,2,0,1:T(4,128)} %reshape_reshape.7, f32[64]{0:T(128)S(1)} %convert_multiply_fusion), kind=kLoop, calls=%fused_computation.23 | loop fusion | flops 8388608 | bytes 25166080 | tf_op jit(solution)/shard_map/convert_element_type | solution.py:66
  328.8 24.4 %copy.57 = bf16[2,1,64,4,8192]{2,3,0,1,4:T(4,128)(2,1)} copy(bf16[2,1,64,4,8192]{4,2,3,1,0:T(8,128)(2,1)} %fusion.16) | data formatting | bytes 16777216 | tf_op jit(solution)/shard_map/convert_element_type | solution.py:66
  353.2 26.5 %reshape.228 = bf16[64,2,32768]{2,1,0:T(2,128)(2,1)} reshape(bf16[8192,1,2,4,64]{4,3,2,1,0:T(4,128)(2,1)} %bitcast.68) | data formatting | bytes 16777216
  379.7 108.5 %all_to_all.15 = bf16[64,2,32768]{2,1,0:T(2,128)(2,1)} all-to-all(bf16[64,2,32768]{2,1,0:T(2,128)(2,1)} %reshape.228), channel_id=1, replica_groups=mesh['inp'=8,'tm'=8,'bl'=2] {'inp','tm'}, dimensions={0} | all-to-all | bytes 16777216 | tf_op jit(solution)/shard_map/all_to_all | solution.py:67
  488.2 26.0 %reshape.229 = bf16[8192,1,2,4,64]{4,3,2,1,0:T(4,128)(2,1)} reshape(bf16[64,2,32768]{2,1,0:T(2,128)(2,1)} %all_to_all.15) | data formatting | bytes 16777216
  514.2 23.4 %copy.77 = bf16[2,1,64,4,64,128]{5,2,3,4,0,1:T(8,128)(2,1)} copy(bf16[2,1,64,4,64,128]{2,3,0,5,4,1:T(4,128)(2,1)} %bitcast.69) | data formatting | bytes 16777216 | tf_op jit(solution)/shard_map/all_to_all | solution.py:67
  537.6 27.8 %reshape.219 = bf16[2,8,8,64,4,2,64]{6,5,3,4,2,1,0:T(2,128)(2,1)} reshape(bf16[2,64,1,64,4,128]{5,3,4,1,0,2:T(8,128)(2,1)} %bitcast.71) | data formatting | bytes 16777216 | tf_op jit(solution)/shard_map/reshape | solution.py:74
  565.4 15.2 %copy.60 = bf16[2,8,8,64,4,2,64]{6,3,2,4,1,0,5:T(8,128)(2,1)} copy(bf16[2,8,8,64,4,2,64]{6,5,3,4,2,1,0:T(2,128)(2,1)} %reshape.219) | data formatting | bytes 16777216 | tf_op jit(solution)/shard_map/reshape | solution.py:74
  580.6 54.9 %all-gather.2.cloned.1.call-done = bf16[2,8,8,128,4,2,64]{6,3,2,4,1,0,5:T(8,128)(2,1)} async-done(((bf16[2,8,8,64,4,2,64]{6,3,2,4,1,0,5:T(8,128)(2,1)}), bf16[2,8,8,128,4,2,64]{6,3,2,4,1,0,5:T(8,128)(2,1)}) %all-gather.2.cloned.1.call-update) | async-done | bytes 16777232 | tf_op jit(solution)/shard_map/all_gather | solution.py:79
  635.4 57.3 %fusion.20 = f32[2,2,2,8,64,8,128]{6,4,3,1,5,2,0:T(8,128)} fusion(bf16[2,8,8,64,4,2,64,1,1]{6,5,3,4,2,1,0,8,7:T(2,128)(2,1)} %bitcast.70, bf16[2,8,8,128,4,2,64]{6,3,2,4,1,0,5:T(8,128)(2,1)} %all-gather.2.cloned.1.call-done), kind=kOutput, calls=%fused_computation.29 | convolution fusion | flops 17179869184 | bytes 41943040 | tf_op jit(solution)/shard_map/xatisgk,yctjsgk->gxyaicj/dot_general | solution.py:76
  692.8 10.4 %slice_add_fusion = (f32[2,1,1,8,64,8,128]{6,4,3,1,5,2,0:T(8,128)}, f32[2,1,1,8,64,8,128]{6,4,3,1,5,2,0:T(8,128)S(1)}) fusion(f32[2,2,2,8,64,8,128]{6,4,3,1,5,2,0:T(8,128)} %fusion.20), kind=kLoop, calls=%fused_computation.33 | loop fusion | flops 2097152 | bytes 25165824 | tf_op jit(solution)/shard_map/add | solution.py:82
  703.1 5.5 copy.62
  713.9 4.4 maximum_multiply_fusion
  (20 shorter events, 10.8 us)
Async XLA Ops:
  6.5 628.9 %all-gather.2.cloned.1.call-start = ((), (), s32[]{:S(2)}) async-start(), calls=%async_computation.1 | async-start | bytes 50331648 | tf_op jit(solution)/shard_map/all_gather | solution.py:79
  14.9 139.2 %collective-permute-start = (bf16[64,3,16384]{2,0,1:T(8,128)(2,1)}, bf16[64,3,16384]{2,0,1:T(8,128)(2,1)}, u32[]{:S(2)}, u32[]{:S(2)}) collective-permute-start(bf16[64,3,16384]{2,0,1:T(8,128)(2,1)} %bitcast.67), channel_id=1, source_target_pairs={{2,0},{4,2},{6,4},{8,6},{10,8},{12,10},{14,12},{3,1},{5,3},{7,5},{... | collective-permute-start | bytes 18874376 | tf_op jit(solution)/shard_map/ppermute | solution.py:13
  27.5 18.5 %copy-start.2 = (s32[64]{0:T(128)S(1)}, s32[64]{0:T(128)}, u32[]{:S(2)}) copy-start(s32[64]{0:T(128)} %param.5) | copy-start | bytes 772
  27.5 18.5 %copy-start.1 = (f32[4,16384]{1,0:T(4,128)S(1)}, f32[4,16384]{1,0:T(4,128)}, u32[]{:S(2)}) copy-start(f32[4,16384]{1,0:T(4,128)} %param.4) | copy-start | bytes 786436
  45.1 120.2 %copy-start = (f32[64,4,16384]{2,1,0:T(4,128)S(1)}, f32[64,4,16384]{2,1,0:T(4,128)}, u32[]{:S(2)}) copy-start(f32[64,4,16384]{2,1,0:T(4,128)} %reshape.218) | copy-start | bytes 50331652
Sparse Core Ops, SparseCore 0:
  580.7 54.6 all-gather.1
where the time goes:
time: 737 us; the launch traced here: 725 us
  local copies, waits for them, and re-layouts  227 us (31%)
  waiting for transfers between devices  163 us (22%)
  matrix products  113 us (15%)
  blocking collectives  108 us (15%)
  other arithmetic  99 us (13%)
  between operations  13.7 us (2%)
    all_to_all x1, blocking collectives, shards(): lax.all_to_all(spectra[:, None], ('inp', 'tm'), split_axis=4, concat_axis...  108 us
    ppermute x1, waiting for transfers between devices, passed_along(): lax.ppermute(value, axis, [(source, source + steps) for source in range(i...  108 us
    dot_general x1, matrix products, shards(): jnp.einsum('xatisgk,yctjsgk->gxyaicj', rows, lax.all_gather(rows, 'bl', a...  57.3 us
    all_gather x1, waiting for transfers between devices, shards(): lax.all_gather(rows, 'bl', axis=3, tiled=True)  54.9 us
    unnamed x8, local copies, waits for them, and re-layouts  52.6 us
    reshape x2, local copies, waits for them, and re-layouts, shards(): turned.reshape(2, groups_inp, groups_tm, inputs, spectra_dev, out_groups,...  43 us
    add x1, other arithmetic, shards(): filtered + taps[offset][None, None, :] * extended[:, offset:offset + spec...  32.6 us
    dot_general x1, matrix products, transform(): jnp.einsum('ykn,mnb->mykb', table_one, blocks, precision=highest)  32.5 us
  transfers between devices with their start and end apart: 2, of which 2 were waited for; matrix products, arithmetic and copies ran while one was open for 4% of the time, Pallas kernels for 0%

commit v1 on v0

--- a/solution.py
+++ b/solution.py
@@ -64,8 +64,14 @@
     both_parts = transform(filtered.reshape(inputs * spectra_dev, length), length)
     scale = flags.astype(jnp.float32)[None, :, None, None] / (8.0 * math.sqrt(length))
     spectra = (both_parts.reshape(2, inputs, spectra_dev, channels) * scale).astype(jnp.bfloat16)
-    turned = lax.all_to_all(
-        spectra[:, None], ("inp", "tm"), split_axis=4, concat_axis=1, tiled=True
+    turned = jnp.concatenate(
+        lax.all_to_all(
+            jnp.stack(jnp.split(spectra[:, None], lax.axis_size(("inp", "tm")), axis=4)),
+            ("inp", "tm"),
+            0,
+            0,
+        ),
+        axis=1,
     )
     groups_inp = lax.axis_size("inp")
     groups_tm = lax.axis_size("tm")

time: 737 us -> 647 us (0.88)
  local copies, waits for them, and re-layouts: 227 us -> 140 us
    unnamed x8 -> x69, local copies, waits for them, and re-layouts: 52.6 us -> 3.12 us
    another operation x0 -> x3, local copies, waits for them, and re-layouts: none -> 43 us  [the longest x2 43 us: shards(): turned.reshape(2, groups_inp, groups_tm, inputs, spectra_dev, out_groups,...]
    reshape x2 -> x1, local copies, waits for them, and re-layouts: 43 us -> 10.7 us  [shards(): jnp.concatenate(lax.all_to_all(jnp.stack(jnp.split(spectra[:, None], lax....]
    convert_element_type x1 -> x0, local copies, waits for them, and re-layouts: 24.4 us -> none  [shards(): (both_parts.reshape(2, inputs, spectra_dev, channels) * scale).astype(jnp...]
    all_to_all x1 -> x0, local copies, waits for them, and re-layouts: 23.4 us -> none  [shards(): lax.all_to_all(spectra[:, None], ('inp', 'tm'), split_axis=4, concat_axis...]
  transfers between devices with their start and end apart: 2 -> 2, of which waited for: 2 -> 2; matrix products, arithmetic and copies ran while one was open for 4% -> 5% of each run, Pallas kernels for 0% -> 0%
where the time goes in v1:
time: 647 us; the launch traced here: 638 us
  waiting for transfers between devices  163 us (25%)
  local copies, waits for them, and re-layouts  140 us (22%)
  matrix products  113 us (17%)
  blocking collectives  108 us (17%)
  other arithmetic  97.7 us (15%)
  between operations  14 us (2%)
    ppermute x1, waiting for transfers between devices, passed_along(): lax.ppermute(value, axis, [(source, source + steps) for source in range(i...  108 us
    all_to_all x1, blocking collectives, shards(): lax.all_to_all(jnp.stack(jnp.split(spectra[:, None], lax.axis_size(('inp'...  108 us
    dot_general x1, matrix products, shards(): jnp.einsum('xatisgk,yctjsgk->gxyaicj', rows, lax.all_gather(rows, 'bl', a...  57.3 us
    all_gather x1, waiting for transfers between devices, shards(): lax.all_gather(rows, 'bl', axis=3, tiled=True)  55.3 us
    another operation x2, local copies, waits for them, and re-layouts, shards(): turned.reshape(2, groups_inp, groups_tm, inputs, spectra_dev, out_groups,...  43 us
    add x1, other arithmetic, shards(): filtered + taps[offset][None, None, :] * extended[:, offset:offset + spec...  32.6 us
    dot_general x1, matrix products, transform(): jnp.einsum('ykn,mnb->mykb', table_one, blocks, precision=highest)  32.5 us
    dot_general x1, matrix products, transform(): jnp.einsum('mxkb,xbyq->ymqk', twisted, table_two, precision=highest)  23.6 us
  transfers between devices with their start and end apart: 2, of which 2 were waited for; matrix products, arithmetic and copies ran while one was open for 5% of the time, Pallas kernels for 0%

profile of v1, /device:TPU:1, one launch (start us, length us, event | category | flops | bytes accessed | tf_op | source)
XLA Modules:
  0.0 637.6 jit_solution(7686779403682112064)
XLA Ops:
  6.5 5.2 slice_convert_fusion
  11.8 3.1 copy.124
  14.9 1.3 collective-permute-start
  16.2 11.3 %convert_element_type.80 = f32[64,65536]{1,0:T(8,128)} convert(s32[64,65536]{1,0:T(8,128)} %param.3) | non-fusion elementwise | flops 4194304 | bytes 33554432 | tf_op jit(solution)/shard_map/convert_element_type | solution.py:54
  27.5 17.6 %reshape.217 = f32[64,4,16384]{2,1,0:T(4,128)} reshape(f32[64,65536]{1,0:T(8,128)} %convert_element_type.80) | data formatting | bytes 33554432 | tf_op jit(solution)/shard_map/reshape | solution.py:54
  46.2 107.9 %collective-permute-done = bf16[64,3,16384]{2,0,1:T(8,128)(2,1)} collective-permute-done((bf16[64,3,16384]{2,0,1:T(8,128)(2,1)}, bf16[64,3,16384]{2,0,1:T(8,128)(2,1)}, u32[]{:S(2)}, u32[]{:S(2)}) %collective-permute-start) | collective-permute-done | bytes 6291488 | tf_op jit(solution)/shard_map/ppermute | solution.py:13
  154.1 11.2 %copy.92 = f32[64,3,16384]{2,1,0:T(4,128)} copy(bf16[64,3,16384]{2,0,1:T(8,128)(2,1)} %collective-permute-done) | data formatting | bytes 18874368 | tf_op jit(solution)/shard_map/convert_element_type | solution.py:57
  165.3 32.6 %fusion.8 = f32[64,4,16384]{2,1,0:T(4,128)} fusion(f32[64,4,16384]{2,1,0:T(4,128)S(1)} %copy-done, f32[64,3,16384]{2,1,0:T(4,128)} %copy.92, f32[16384]{0:T(1024)S(1)} %bitcast.327, f32[16384]{0:T(1024)S(1)} %bitcast.328, f32[16384]{0:T(1024)S(1)} %bitcast.326, f32[16384]{0:T(1024)S(1)} %bitcast.325), kind=kLoop, calls=%fused_computation.13 | loop fusion | flops 41943040 | bytes 46399488 | tf_op jit(solution)/shard_map/add | solution.py:61
  197.9 20.5 %reshape_reshape.9 = f32[256,128,128]{2,1,0:T(8,128)} reshape(f32[64,4,16384]{2,1,0:T(4,128)} %fusion.8) | data formatting | bytes 33554432 | tf_op jit(solution)/shard_map/reshape;reshape | solution.py:29
  218.4 32.5 %fusion.17 = f32[256,2,128,128]{2,3,1,0:T(8,128)} fusion(f32[256,128,128]{2,1,0:T(8,128)} %reshape_reshape.9, f32[1,128,128]{2,1,0:T(8,128)S(1)} %get-tuple-element.15, f32[1,128,128]{2,1,0:T(8,128)S(1)} %get-tuple-element.16), kind=kOutput, calls=%fused_computation.26 | convolution fusion | flops 12884934656 | bytes 50462720 | tf_op jit(solution)/shard_map/ykn,mnb->mykb/dot_general | solution.py:32
  250.8 17.8 %multiply_add_fusion = (f32[256,1,128,128]{2,3,1,0:T(8,128)S(1)}, f32[256,1,128,128]{2,3,1,0:T(8,128)}) fusion(f32[256,2,128,128]{2,3,1,0:T(8,128)} %fusion.17, f32[128,128]{0,1:T(8,128)S(1)} %get-tuple-element.17, f32[128,128]{0,1:T(8,128)S(1)} %get-tuple-element.18), kind=kLoop, calls=%fused_computation.25 | loop fusion | flops 25165824 | bytes 67239936 | tf_op jit(solution)/shard_map/add | solution.py:37
  268.6 23.6 %fusion.25 = f32[2,256,64,128]{3,2,1,0:T(8,128)} fusion(f32[256,1,128,128]{2,3,1,0:T(8,128)} %get-tuple-element.6, f32[256,1,128,128]{2,3,1,0:T(8,128)S(1)} %get-tuple-element.5, f32[1,128,2,64]{1,3,0,2:T(8,128)S(1)} %get-tuple-element.14, f32[1,128,2,64]{1,3,0,2:T(8,128)S(1)} %get-tuple-element.13), kind=kOutput, calls=%fused_computation.30 | convolution fusion | flops 12893323264 | bytes 50462720 | tf_op jit(solution)/shard_map/mxkb,xbyq->ymqk/dot_general | solution.py:44
  292.2 19.9 %reshape_reshape.10 = f32[2,1,64,4,8192]{4,3,2,0,1:T(4,128)} reshape(f32[2,256,64,128]{3,2,1,0:T(8,128)} %fusion.25) | data formatting | bytes 33554432 | tf_op jit(solution)/shard_map/reshape;reshape | solution.py:66
  312.2 15.3 %fusion.16 = bf16[2,1,64,4,8192]{4,2,3,0,1:T(8,128)(2,1)S(1)} fusion(f32[2,1,64,4,8192]{4,3,2,0,1:T(4,128)} %reshape_reshape.10, f32[64]{0:T(128)S(1)} %convert_multiply_fusion), kind=kLoop, calls=%fused_computation.23 | loop fusion | flops 8388608 | bytes 25166080 | tf_op jit(solution)/shard_map/convert_element_type | solution.py:66
  330.9 107.9 %all_to_all.5 = bf16[64,2,1,64,4,128]{5,3,4,1,2,0:T(8,128)(2,1)} all-to-all(bf16[64,2,1,64,4,128]{5,3,4,1,2,0:T(8,128)(2,1)S(1)} %constant_dynamic-update-slice_fusion), channel_id=1, replica_groups=mesh['inp'=8,'tm'=8,'bl'=2] {'inp','tm'}, dimensions={0} | all-to-all | bytes 16777216 | tf_op jit(solution)/shard_map/all_to_all | solution.py:68
  438.7 10.7 %copy.96 = bf16[2,64,1,64,4,128]{5,3,4,1,0,2:T(8,128)(2,1)} copy(bf16[2,64,1,64,4,128]{5,3,4,0,2,1:T(8,128)(2,1)} %bitcast.321) | data formatting | bytes 16777216 | tf_op jit(solution)/shard_map/reshape | solution.py:67
  449.4 27.8 %reshape_reshape.11 = bf16[2,8,8,64,4,2,64]{6,5,3,4,2,1,0:T(2,128)(2,1)} reshape(bf16[2,64,1,64,4,128]{5,3,4,1,0,2:T(8,128)(2,1)} %copy.96) | data formatting | bytes 16777216 | tf_op jit(solution)/shard_map/reshape;reshape | solution.py:80
  477.2 15.2 %copy.97 = bf16[2,8,8,64,4,2,64]{6,3,2,4,1,0,5:T(8,128)(2,1)} copy(bf16[2,8,8,64,4,2,64]{6,5,3,4,2,1,0:T(2,128)(2,1)} %reshape_reshape.11) | data formatting | bytes 16777216 | tf_op jit(solution)/shard_map/reshape;reshape | solution.py:80
  492.4 55.3 %all-gather.2.cloned.1.call-done = bf16[2,8,8,128,4,2,64]{6,3,2,4,1,0,5:T(8,128)(2,1)} async-done(((bf16[2,8,8,64,4,2,64]{6,3,2,4,1,0,5:T(8,128)(2,1)}), bf16[2,8,8,128,4,2,64]{6,3,2,4,1,0,5:T(8,128)(2,1)}) %all-gather.2.cloned.1.call-update) | async-done | bytes 16777232 | tf_op jit(solution)/shard_map/all_gather | solution.py:85
  547.7 57.3 %fusion.20 = f32[2,2,2,8,64,8,128]{6,4,3,1,5,2,0:T(8,128)} fusion(bf16[2,8,8,64,4,2,64,1,1]{6,5,3,4,2,1,0,8,7:T(2,128)(2,1)} %bitcast.320, bf16[2,8,8,128,4,2,64]{6,3,2,4,1,0,5:T(8,128)(2,1)} %all-gather.2.cloned.1.call-done), kind=kOutput, calls=%fused_computation.29 | convolution fusion | flops 17179869184 | bytes 41943040 | tf_op jit(solution)/shard_map/xatisgk,yctjsgk->gxyaicj/dot_general | solution.py:82
  605.0 10.4 %slice_add_fusion = (f32[2,1,1,8,64,8,128]{6,4,3,1,5,2,0:T(8,128)}, f32[2,1,1,8,64,8,128]{6,4,3,1,5,2,0:T(8,128)S(1)}) fusion(f32[2,2,2,8,64,8,128]{6,4,3,1,5,2,0:T(8,128)} %fusion.20), kind=kLoop, calls=%fused_computation.33 | loop fusion | flops 2097152 | bytes 25165824 | tf_op jit(solution)/shard_map/add | solution.py:88
  615.4 5.5 copy.99
  621.9 3.3 copy.100
  626.2 4.4 maximum_multiply_fusion
  (81 shorter events, 6.2 us)
Async XLA Ops:
  6.5 541.2 %all-gather.2.cloned.1.call-start = ((), (), s32[]{:S(2)}) async-start(), calls=%async_computation.1 | async-start | bytes 50331648 | tf_op jit(solution)/shard_map/all_gather | solution.py:85
  14.9 139.2 %collective-permute-start = (bf16[64,3,16384]{2,0,1:T(8,128)(2,1)}, bf16[64,3,16384]{2,0,1:T(8,128)(2,1)}, u32[]{:S(2)}, u32[]{:S(2)}) collective-permute-start(bf16[64,3,16384]{2,0,1:T(8,128)(2,1)} %bitcast.319), channel_id=1, source_target_pairs={{2,0},{4,2},{6,4},{8,6},{10,8},{12,10},{14,12},{3,1},{5,3},{7,5},{... | collective-permute-start | bytes 18874376 | tf_op jit(solution)/shard_map/ppermute | solution.py:13
  27.5 18.5 %copy-start.2 = (s32[64]{0:T(128)S(1)}, s32[64]{0:T(128)}, u32[]{:S(2)}) copy-start(s32[64]{0:T(128)} %param.5) | copy-start | bytes 772
  27.5 18.5 %copy-start.1 = (f32[4,16384]{1,0:T(4,128)S(1)}, f32[4,16384]{1,0:T(4,128)}, u32[]{:S(2)}) copy-start(f32[4,16384]{1,0:T(4,128)} %param.4) | copy-start | bytes 786436
  46.2 119.1 %copy-start = (f32[64,4,16384]{2,1,0:T(4,128)S(1)}, f32[64,4,16384]{2,1,0:T(4,128)}, u32[]{:S(2)}) copy-start(f32[64,4,16384]{2,1,0:T(4,128)} %reshape.217) | copy-start | bytes 50331652
Sparse Core Ops, SparseCore 0:
  492.6 55.1 all-gather.1
